TPU v7x, 512 devices: a whole 4x8x8 slice. The times are simulated.
512 devices in a mesh: panel: 2 (over y_lo), lon: 16 (over z, core), lat: 16 (over y_hi, x).
Axes of the slice: x: 4, y: 8 (y_hi: 4, y_lo: 2; y = y_hi * 2 + y_lo), z: 8, core: 2. Of those that a mesh axis runs over, the one named last changes fastest.
Arguments:
- pressure: float32 [2, 256, 512, 128], P('panel', 'lat', 'lon'), may hold values from -6 to 6
- porosity: float32 [2, 256, 512, 128], P('panel', 'lat', 'lon'), may hold values from 0.5 to 2
- source: float32 [2, 256, 512, 128], P('panel', 'lat', 'lon'), may hold values from -6 to 6
- bulk: float32 [2, 256, 512, 128], P('panel', 'lat', 'lon'), may hold values from 0.5 to 2
- lat_codes: int32 [2, 2, 2, 512], P('panel', None, None, 'lon'), may hold values from 0 to 8158, as said below
- lat_weights: float32 [2, 4, 2, 2, 512], P('panel', None, None, None, 'lon'), may hold values from 0 to 1, as said below
- lon_codes: int32 [2, 2, 2, 256], P('panel', None, None, 'lat'), may hold values from 0 to 8174, as said below
- lon_weights: float32 [2, 4, 2, 2, 256], P('panel', None, None, None, 'lat'), may hold values from 0 to 1, as said below
Outputs:
- pressure_out: float32 [2, 256, 512, 128], P('panel', 'lat', 'lon')
- porosity_out: float32 [2, 256, 512, 128], P('panel', 'lat', 'lon')
Inputs may be any that keep to these rules, and one draw needn't show every extreme that they name: `lat_codes`: an intersection map of the shell, which may differ from draw to draw: code = a * 32 + c with a < 255 a latitude of the whole panel and c < 31 an offset inside the longitude block of the ghost cell. `lon_codes`: an intersection map of the shell, which may differ from draw to draw: code = b * 16 + r with b < 511 a longitude of the whole panel and r < 15 an offset inside the latitude block of the ghost cell. `lat_weights`: the four weights of a ghost cell are non-negative and sum to one. `lon_weights`: the four weights of a ghost cell are non-negative and sum to one.
All inputs are finite; a program needn't handle non-finite values.
Results may differ from a plain program's by a relative error of at most 0.0003.
Values sent between devices are 32-bit elements; how exact they have to be, the bound alone decides.
A program may use at most 64 MiB of HBM per device.

v0:
```python
import jax
import jax.numpy as jnp
from jax import lax
from jax.sharding import PartitionSpec as P

SWEEPS = 3
stencil_offsets = ((0, 0), (0, 1), (1, 0), (1, 1))
radial_weight = 0.25
buoyancy = 0.5
time_step = 0.04


def padded_2(cells, sides, width):
    for axis, dim in sides:
        count = lax.axis_size(axis)
        ends = count - 1
        head = lax.slice_in_dim(cells, 0, width, axis=dim)
        tail = lax.slice_in_dim(cells, cells.shape[dim] - width, cells.shape[dim], axis=dim)
        cells = jnp.concatenate(
            [
                lax.ppermute(tail, axis, [(i, (i + 1) % count) for i in range(ends)]),
                cells,
                lax.ppermute(head, axis, [((i + 1) % count, i) for i in range(ends)]),
            ],
            axis=dim,
        )
    return cells


def swapped(block, axis, distance):
    count = lax.axis_size(axis)
    route = []
    for low in range(count):
        high = low | 1 << distance
        if high != low and high < count:
            route += [(low, high), (high, low)]
    return lax.ppermute(block, axis, route)


def pad_last(values, before, after):
    widths = [(0, 0)] * (values.ndim - 1) + [(before, after)]
    return jnp.pad(values, widths)


def rim_terms(field, lat_codes, lat_weights, lon_codes, lon_weights, width):
    rows_dev, cols_dev, levels = field.shape
    first_row = lax.axis_index("lat") * rows_dev
    first_col = lax.axis_index("lon") * cols_dev
    chosen = lat_codes[:, :width]
    rows_at = chosen // cols_dev - first_row
    cols_at = chosen % cols_dev
    lat_total = jnp.zeros(chosen.shape + (levels,), jnp.float32)
    for corner, (row_step, col_step) in enumerate(stencil_offsets):
        target = rows_at + row_step
        inside = (target >= 0) & (target < rows_dev)
        picked = field[jnp.clip(target, 0, rows_dev - 1), cols_at + col_step]
        lat_total = (
            lat_total + jnp.where(inside, lat_weights[corner, :, :width], 0.0)[..., None] * picked
        )
    chosen = lon_codes[:, :width]
    cols_at = chosen // rows_dev - first_col
    rows_at = chosen % rows_dev
    lon_total = jnp.zeros(chosen.shape + (levels,), jnp.float32)
    for corner, (row_step, col_step) in enumerate(stencil_offsets):
        target = cols_at + col_step
        inside = (target >= 0) & (target < cols_dev)
        picked = field[rows_at + row_step, jnp.clip(target, 0, cols_dev - 1)]
        lon_total = (
            lon_total + jnp.where(inside, lon_weights[corner, :, :width], 0.0)[..., None] * picked
        )
    return (lat_total, lon_total)


def surround(field, width, lat_codes, lat_weights, lon_codes, lon_weights):
    rows_dev, cols_dev, levels = field.shape
    padded = padded_2(field, (("lat", 0), ("lon", 1)), width)
    lat_terms, lon_terms = rim_terms(field, lat_codes, lat_weights, lon_codes, lon_weights, width)
    lat_summed = lax.psum(lat_terms, "lat")
    lon_summed = lax.psum(lon_terms, "lon")
    arrived = swapped(jnp.concatenate([lat_summed, lon_summed], axis=2), "panel", 0)
    lat_rim = arrived[:, :, :cols_dev]
    lon_rim = arrived[:, :, cols_dev:]
    lat_index = lax.axis_index("lat")
    lon_index = lax.axis_index("lon")
    last_lat = lax.axis_size("lat") - 1
    last_lon = lax.axis_size("lon") - 1
    north = jnp.where(lat_index == 0, lat_rim[0][::-1], padded[:width, width : width + cols_dev])
    padded = padded.at[:width, width : width + cols_dev].set(north)
    south = jnp.where(
        lat_index == last_lat, lat_rim[1], padded[width + rows_dev :, width : width + cols_dev]
    )
    padded = padded.at[width + rows_dev :, width : width + cols_dev].set(south)
    west = jnp.where(
        lon_index == 0,
        jnp.moveaxis(lon_rim[0][::-1], 0, 1),
        padded[width : width + rows_dev, :width],
    )
    padded = padded.at[width : width + rows_dev, :width].set(west)
    east = jnp.where(
        lon_index == last_lon,
        jnp.moveaxis(lon_rim[1], 0, 1),
        padded[width : width + rows_dev, width + cols_dev :],
    )
    padded = padded.at[width : width + rows_dev, width + cols_dev :].set(east)
    return padded


def face_terms(mobility):
    lat_face = 0.5 * (mobility[..., :-1, 1:-1, :] + mobility[..., 1:, 1:-1, :])
    lon_face = 0.5 * (mobility[..., 1:-1, :-1, :] + mobility[..., 1:-1, 1:, :])
    inner = mobility[..., 1:-1, 1:-1, :]
    mean_rad = 0.5 * (inner[..., :-1] + inner[..., 1:])
    return (lat_face, lon_face, mean_rad)


def diagonal_sum(bulk, lat_face, lon_face, mean_rad):
    rad_face = radial_weight * mean_rad
    total = bulk + lat_face[..., :-1, :, :] + lat_face[..., 1:, :, :]
    total = total + lon_face[..., :, :-1, :] + lon_face[..., :, 1:, :]
    return total + pad_last(rad_face, 1, 0) + pad_last(rad_face, 0, 1)


def neighbour_total(padded, source, lat_face, lon_face, mean_rad):
    inner = padded[..., 1:-1, 1:-1, :]
    rad_face = radial_weight * mean_rad
    total = source + lat_face[..., :-1, :, :] * padded[..., :-2, 1:-1, :]
    total = total + lat_face[..., 1:, :, :] * padded[..., 2:, 1:-1, :]
    total = total + lon_face[..., :, :-1, :] * padded[..., 1:-1, :-2, :]
    total = total + lon_face[..., :, 1:, :] * padded[..., 1:-1, 2:, :]
    total = (
        total
        + pad_last(rad_face * inner[..., :-1], 1, 0)
        + pad_last(rad_face * inner[..., 1:], 0, 1)
    )
    return total


def advect(pressure_pad, porosity_pad, lat_face, lon_face, mean_rad, bulk):
    pressure_in = pressure_pad[..., 1:-1, 1:-1, :]
    porosity_in = porosity_pad[..., 2:-2, 2:-2, :]
    lat_speed = -lat_face * (pressure_pad[..., 1:, 1:-1, :] - pressure_pad[..., :-1, 1:-1, :])
    lat_left = 1.5 * porosity_pad[..., 1:-2, 2:-2, :] - 0.5 * porosity_pad[..., :-3, 2:-2, :]
    lat_right = 1.5 * porosity_pad[..., 2:-1, 2:-2, :] - 0.5 * porosity_pad[..., 3:, 2:-2, :]
    lat_flux = lat_speed * jnp.where(lat_speed > 0, lat_left, lat_right)
    lon_speed = -lon_face * (pressure_pad[..., 1:-1, 1:, :] - pressure_pad[..., 1:-1, :-1, :])
    lon_left = 1.5 * porosity_pad[..., 2:-2, 1:-2, :] - 0.5 * porosity_pad[..., 2:-2, :-3, :]
    lon_right = 1.5 * porosity_pad[..., 2:-2, 2:-1, :] - 0.5 * porosity_pad[..., 2:-2, 3:, :]
    lon_flux = lon_speed * jnp.where(lon_speed > 0, lon_left, lon_right)
    rad_speed = (
        -radial_weight * mean_rad * (pressure_in[..., 1:] - pressure_in[..., :-1])
        + buoyancy * mean_rad
    )
    rad_flux = rad_speed * jnp.where(rad_speed > 0, porosity_in[..., :-1], porosity_in[..., 1:])
    divergence = lat_flux[..., 1:, :, :] - lat_flux[..., :-1, :, :]
    divergence = divergence + lon_flux[..., :, 1:, :] - lon_flux[..., :, :-1, :]
    divergence = divergence + pad_last(rad_flux, 0, 1) - pad_last(rad_flux, 1, 0)
    return porosity_in - time_step * (divergence + bulk * pressure_in)


def body(pressure, porosity, source, bulk, lat_codes, lat_weights, lon_codes, lon_weights):
    current = pressure[0]
    porosity_now = porosity[0]
    source_now = source[0]
    bulk_now = bulk[0]
    lat_code_now = lat_codes[0]
    lat_weight_now = lat_weights[0]
    lon_code_now = lon_codes[0]
    lon_weight_now = lon_weights[0]
    levels = porosity_now.shape[-1]
    both_pad = surround(
        jnp.concatenate([porosity_now, current], axis=-1),
        2,
        lat_code_now,
        lat_weight_now,
        lon_code_now,
        lon_weight_now,
    )
    porosity_pad = both_pad[..., :levels]
    first_pad = both_pad[1:-1, 1:-1, levels:]
    near = porosity_pad[1:-1, 1:-1, :]
    mobility = near * near * near
    lat_face, lon_face, mean_rad = face_terms(mobility)
    denominator = diagonal_sum(bulk_now, lat_face, lon_face, mean_rad)
    for sweep_index in range(SWEEPS):
        if sweep_index == 0:
            padded = first_pad
        else:
            padded = surround(
                current, 1, lat_code_now, lat_weight_now, lon_code_now, lon_weight_now
            )
        current = neighbour_total(padded, source_now, lat_face, lon_face, mean_rad) / denominator
    pressure_pad = surround(current, 1, lat_code_now, lat_weight_now, lon_code_now, lon_weight_now)
    porosity_new = advect(pressure_pad, porosity_pad, lat_face, lon_face, mean_rad, bulk_now)
    return (current[None], porosity_new[None])


def solution(mesh):
    placed = (
        P("panel", "lat", "lon", None),
        P("panel", "lat", "lon", None),
        P("panel", "lat", "lon", None),
        P("panel", "lat", "lon", None),
        P("panel", None, None, "lon"),
        P("panel", None, None, None, "lon"),
        P("panel", None, None, "lat"),
        P("panel", None, None, None, "lat"),
    )
    return jax.shard_map(
        body,
        mesh=mesh,
        in_specs=placed,
        out_specs=(P("panel", "lat", "lon", None), P("panel", "lat", "lon", None)),
        check_vma=False,
    )
```

profile of v0, /device:TPU:296, one launch (start us, length us, event | category | flops | bytes accessed | tf_op | source)
XLA Modules:
  0.0 794.1 jit_solution(9546006194397543275)
XLA Ops:
  7.2 1.3 copy_bitcast_fusion
  8.6 3.4 collective-permute-start
  12.0 6.7 collective-permute-start.1
  20.1 0.9 gather_fusion.7
  21.0 0.9 gather_fusion.6
  21.9 0.9 gather_fusion.5
  22.9 0.9 gather_fusion.4
  25.6 1.3 gather_fusion.3
  26.9 1.3 gather_fusion.2
  28.2 1.3 gather_fusion.1
  29.5 1.3 gather_fusion
  33.9 1.9 collective-permute-start.2
  35.9 4.9 collective-permute-start.3
  40.7 85.8 %all-reduce.15.cloned.1.call-done = f32[2,2,16,256]{3,2,1,0:T(8,128)} async-done(((f32[2,2,16,256]{3,2,1,0:T(8,128)}), f32[2,2,16,256]{3,2,1,0:T(8,128)}) %all-reduce.15.cloned.1.call-update) | async-done | bytes 65552 | tf_op jit(solution)/shard_map/psum | solution.py:79
  126.6 174.8 %all-reduce.13.cloned.1.call-done = f32[2,2,32,256]{3,2,1,0:T(8,128)} async-done(((f32[2,2,32,256]{3,2,1,0:T(8,128)}), f32[2,2,32,256]{3,2,1,0:T(8,128)}) %all-reduce.13.cloned.1.call-update) | async-done | bytes 131088 | tf_op jit(solution)/shard_map/psum | solution.py:78
  301.3 1.0 pad_maximum_fusion.5
  302.3 3.4 collective-permute-start.4
  307.0 2.8 collective-permute-done.4
  310.2 1.9 dynamic-slice_select_fusion
  312.1 1.7 scatter.54
  316.4 6.1 collective-permute-start.6
  325.3 1.9 collective-permute-start.5
  327.3 0.9 gather_fusion.11
  330.9 82.9 %psum.58 = f32[2,1,32,128]{3,2,1,0:T(8,128)S(1)} all-reduce(f32[2,1,32,128]{3,2,1,0:T(8,128)S(1)} %multiply_add_fusion.4), channel_id=1, replica_groups=mesh['panel'=2,'lon'=16,'lat'=16] {'lat'}, use_global_device_ids=true, to_apply=%region_3.4 | all-reduce | flops 8192 | bytes 65536 | tf_op jit(solution)/shard_map/psum | solution.py:78
  413.9 45.7 %psum.59 = f32[2,1,16,128]{3,2,1,0:T(8,128)S(1)} all-reduce(f32[2,1,16,128]{3,2,1,0:T(8,128)S(1)} %multiply_add_fusion.7), channel_id=1, replica_groups=mesh['panel'=2,'lon'=16,'lat'=16] {'lon'}, use_global_device_ids=true, to_apply=%region_4.5 | all-reduce | flops 4096 | bytes 32768 | tf_op jit(solution)/shard_map/psum | solution.py:79
  459.6 2.1 collective-permute-start.7
  461.8 4.9 collective-permute-start.8
  466.6 2.4 collective-permute-start.9
  469.2 3.5 collective-permute-done.9
  472.6 1.4 scatter.60
  482.5 1.9 collective-permute-start.11
  484.5 3.9 collective-permute-start.10
  488.5 80.9 %psum.60 = f32[2,1,32,128]{3,2,1,0:T(8,128)S(1)} all-reduce(f32[2,1,32,128]{3,2,1,0:T(8,128)S(1)} %multiply_add_fusion.3), channel_id=1, replica_groups=mesh['panel'=2,'lon'=16,'lat'=16] {'lat'}, use_global_device_ids=true, to_apply=%region_5.6 | all-reduce | flops 8192 | bytes 65536 | tf_op jit(solution)/shard_map/psum | solution.py:78
  569.5 45.7 %psum.61 = f32[2,1,16,128]{3,2,1,0:T(8,128)S(1)} all-reduce(f32[2,1,16,128]{3,2,1,0:T(8,128)S(1)} %multiply_add_fusion.6), channel_id=1, replica_groups=mesh['panel'=2,'lon'=16,'lat'=16] {'lon'}, use_global_device_ids=true, to_apply=%region_6.7 | all-reduce | flops 4096 | bytes 32768 | tf_op jit(solution)/shard_map/psum | solution.py:79
  615.2 1.9 collective-permute-start.12
  617.2 4.9 collective-permute-start.13
  622.0 2.4 collective-permute-start.14
  624.6 3.5 collective-permute-done.14
  628.0 1.4 scatter.66
  638.0 1.9 collective-permute-start.16
  639.9 3.9 collective-permute-start.15
  643.9 80.9 %psum.62 = f32[2,1,32,128]{3,2,1,0:T(8,128)S(1)} all-reduce(f32[2,1,32,128]{3,2,1,0:T(8,128)S(1)} %multiply_add_fusion.2), channel_id=1, replica_groups=mesh['panel'=2,'lon'=16,'lat'=16] {'lat'}, use_global_device_ids=true, to_apply=%region_7.8 | all-reduce | flops 8192 | bytes 65536 | tf_op jit(solution)/shard_map/psum | solution.py:78
  724.9 45.7 %psum.63 = f32[2,1,16,128]{3,2,1,0:T(8,128)S(1)} all-reduce(f32[2,1,16,128]{3,2,1,0:T(8,128)S(1)} %multiply_add_fusion.5), channel_id=1, replica_groups=mesh['panel'=2,'lon'=16,'lat'=16] {'lon'}, use_global_device_ids=true, to_apply=%region_8.9 | all-reduce | flops 4096 | bytes 32768 | tf_op jit(solution)/shard_map/psum | solution.py:79
  770.7 1.9 collective-permute-start.17
  772.6 4.9 collective-permute-start.18
  777.5 2.4 collective-permute-start.19
  780.8 2.7 collective-permute-done.19
  783.4 1.4 scatter.74
  (194 shorter events, 36.7 us)
Async XLA Ops:
  7.2 119.4 %all-reduce.15.cloned.1.call-start = ((), (), s32[]{:S(2)}) async-start(), calls=%async_computation.1 | async-start | bytes 131072 | tf_op jit(solution)/shard_map/psum | solution.py:79
  8.6 25.3 %collective-permute-start = (f32[2,32,256]{2,0,1:T(2,128)S(1)}, f32[2,32,256]{2,0,1:T(2,128)S(1)}, u32[]{:S(2)}, u32[]{:S(2)}) collective-permute-start(f32[2,32,256]{2,0,1:T(2,128)S(1)} %get-tuple-element.224), channel_id=1, source_target_pairs={{0,1},{1,2},{2,3},{3,4},{4,5},{5,6},{6,7},{7,8},{8,9},{9,10},{10,1... | collective-permute-start | bytes 196616 | tf_op jit(solution)/shard_map/ppermute | solution.py:21
  12.0 21.9 %collective-permute-start.1 = (f32[2,32,256]{2,0,1:T(2,128)S(1)}, f32[2,32,256]{2,0,1:T(2,128)S(1)}, u32[]{:S(2)}, u32[]{:S(2)}) collective-permute-start(f32[2,32,256]{2,0,1:T(2,128)S(1)} %get-tuple-element.225), channel_id=1, source_target_pairs={{1,0},{2,1},{3,2},{4,3},{5,4},{6,5},{7,6},{8,7},{9,8},{10,9},{11,1... | collective-permute-start | bytes 196616 | tf_op jit(solution)/shard_map/ppermute | solution.py:23
  18.7 0.7 copy-start.6
  18.7 0.7 copy-start.4
  24.5 0.7 copy-start.7
  24.5 0.7 copy-start.5
  24.5 276.8 %all-reduce.13.cloned.1.call-start = ((), (), s32[]{:S(2)}) async-start(), calls=%async_computation | async-start | bytes 262144 | tf_op jit(solution)/shard_map/psum | solution.py:78
  31.9 0.7 copy-start.8
  33.9 273.0 %collective-permute-start.2 = (f32[20,2,256]{2,0,1:T(8,128)S(1)}, f32[20,2,256]{2,0,1:T(8,128)S(1)}, u32[]{:S(2)}, u32[]{:S(2)}) collective-permute-start(f32[20,2,256]{2,0,1:T(8,128)S(1)} %get-tuple-element.222), channel_id=1, source_target_pairs={{0,16},{16,32},{32,48},{48,64},{64,80},{80,96},{96,112},{112,128},... | collective-permute-start | bytes 122888 | tf_op jit(solution)/shard_map/ppermute | solution.py:21
  35.9 271.0 %collective-permute-start.3 = (f32[20,2,256]{2,0,1:T(8,128)S(1)}, f32[20,2,256]{2,0,1:T(8,128)S(1)}, u32[]{:S(2)}, u32[]{:S(2)}) collective-permute-start(f32[20,2,256]{2,0,1:T(8,128)S(1)} %get-tuple-element.223), channel_id=1, source_target_pairs={{16,0},{32,16},{48,32},{64,48},{80,64},{96,80},{112,96},{128,112},... | collective-permute-start | bytes 122888 | tf_op jit(solution)/shard_map/ppermute | solution.py:23
  302.3 7.6 collective-permute-start.4
  314.7 1.0 copy-start
  314.7 1.0 copy-start.1
  316.4 143.2 %collective-permute-start.6 = (f32[1,32,128]{2,0,1:T(1,128)S(1)}, f32[1,32,128]{2,0,1:T(1,128)S(1)}, u32[]{:S(2)}, u32[]{:S(2)}) collective-permute-start(f32[1,32,128]{2,0,1:T(1,128)S(1)} %slice.1083), channel_id=1, source_target_pairs={{1,0},{2,1},{3,2},{4,3},{5,4},{6,5},{7,6},{8,7},{9,8},{10,9},{11,1... | collective-permute-start | bytes 49160 | tf_op jit(solution)/shard_map/ppermute | solution.py:23
  325.3 134.3 %collective-permute-start.5 = (f32[1,32,128]{2,1,0:T(8,128)S(1)}, f32[1,32,128]{2,1,0:T(8,128)S(1)}, u32[]{:S(2)}, u32[]{:S(2)}) collective-permute-start(f32[1,32,128]{2,1,0:T(8,128)S(1)} %slice.1082), channel_id=1, source_target_pairs={{0,1},{1,2},{2,3},{3,4},{4,5},{5,6},{6,7},{7,8},{8,9},{9,10},{10,1... | collective-permute-start | bytes 49160 | tf_op jit(solution)/shard_map/ppermute | solution.py:21
  459.6 9.4 %collective-permute-start.7 = (f32[18,1,128]{2,0,1:T(8,128)S(1)}, f32[18,1,128]{2,0,1:T(8,128)S(1)}, u32[]{:S(2)}, u32[]{:S(2)}) collective-permute-start(f32[18,1,128]{2,0,1:T(8,128)S(1)} %get-tuple-element.230), channel_id=1, source_target_pairs={{0,16},{16,32},{32,48},{48,64},{64,80},{80,96},{96,112},{112,128},... | collective-permute-start | bytes 27656 | tf_op jit(solution)/shard_map/ppermute | solution.py:21
  461.8 7.3 collective-permute-start.8
  466.6 6.0 collective-permute-start.9
  474.6 1.0 copy-start.2
  482.5 132.7 %collective-permute-start.11 = (f32[1,32,128]{2,0,1:T(1,128)S(1)}, f32[1,32,128]{2,0,1:T(1,128)S(1)}, u32[]{:S(2)}, u32[]{:S(2)}) collective-permute-start(f32[1,32,128]{2,0,1:T(1,128)S(1)} %slice.1124), channel_id=1, source_target_pairs={{1,0},{2,1},{3,2},{4,3},{5,4},{6,5},{7,6},{8,7},{9,8},{10,9},{11,1... | collective-permute-start | bytes 49160 | tf_op jit(solution)/shard_map/ppermute | solution.py:23
  484.5 130.7 %collective-permute-start.10 = (f32[1,32,128]{2,1,0:T(8,128)S(1)}, f32[1,32,128]{2,1,0:T(8,128)S(1)}, u32[]{:S(2)}, u32[]{:S(2)}) collective-permute-start(f32[1,32,128]{2,1,0:T(8,128)S(1)} %slice.1123), channel_id=1, source_target_pairs={{0,1},{1,2},{2,3},{3,4},{4,5},{5,6},{6,7},{7,8},{8,9},{9,10},{10,1... | collective-permute-start | bytes 49160 | tf_op jit(solution)/shard_map/ppermute | solution.py:21
  615.2 9.2 %collective-permute-start.12 = (f32[18,1,128]{2,0,1:T(8,128)S(1)}, f32[18,1,128]{2,0,1:T(8,128)S(1)}, u32[]{:S(2)}, u32[]{:S(2)}) collective-permute-start(f32[18,1,128]{2,0,1:T(8,128)S(1)} %get-tuple-element.228), channel_id=1, source_target_pairs={{0,16},{16,32},{32,48},{48,64},{64,80},{80,96},{96,112},{112,128},... | collective-permute-start | bytes 27656 | tf_op jit(solution)/shard_map/ppermute | solution.py:21
  617.2 7.3 collective-permute-start.13
  622.0 6.0 collective-permute-start.14
  630.0 1.0 copy-start.3
  638.0 132.7 %collective-permute-start.16 = (f32[1,32,128]{2,0,1:T(1,128)S(1)}, f32[1,32,128]{2,0,1:T(1,128)S(1)}, u32[]{:S(2)}, u32[]{:S(2)}) collective-permute-start(f32[1,32,128]{2,0,1:T(1,128)S(1)} %slice.1140), channel_id=1, source_target_pairs={{1,0},{2,1},{3,2},{4,3},{5,4},{6,5},{7,6},{8,7},{9,8},{10,9},{11,1... | collective-permute-start | bytes 49160 | tf_op jit(solution)/shard_map/ppermute | solution.py:23
  639.9 130.7 %collective-permute-start.15 = (f32[1,32,128]{2,1,0:T(8,128)S(1)}, f32[1,32,128]{2,1,0:T(8,128)S(1)}, u32[]{:S(2)}, u32[]{:S(2)}) collective-permute-start(f32[1,32,128]{2,1,0:T(8,128)S(1)} %slice.1139), channel_id=1, source_target_pairs={{0,1},{1,2},{2,3},{3,4},{4,5},{5,6},{6,7},{7,8},{8,9},{9,10},{10,1... | collective-permute-start | bytes 49160 | tf_op jit(solution)/shard_map/ppermute | solution.py:21
  770.7 10.0 %collective-permute-start.17 = (f32[18,1,128]{2,0,1:T(8,128)S(1)}, f32[18,1,128]{2,0,1:T(8,128)S(1)}, u32[]{:S(2)}, u32[]{:S(2)}) collective-permute-start(f32[18,1,128]{2,0,1:T(8,128)S(1)} %get-tuple-element.226), channel_id=1, source_target_pairs={{0,16},{16,32},{32,48},{48,64},{64,80},{80,96},{96,112},{112,128},... | collective-permute-start | bytes 27656 | tf_op jit(solution)/shard_map/ppermute | solution.py:21
  772.6 8.1 %collective-permute-start.18 = (f32[18,1,128]{2,0,1:T(8,128)S(1)}, f32[18,1,128]{2,0,1:T(8,128)S(1)}, u32[]{:S(2)}, u32[]{:S(2)}) collective-permute-start(f32[18,1,128]{2,0,1:T(8,128)S(1)} %get-tuple-element.227), channel_id=1, source_target_pairs={{16,0},{32,16},{48,32},{64,48},{80,64},{96,80},{112,96},{128,112},... | collective-permute-start | bytes 27656 | tf_op jit(solution)/shard_map/ppermute | solution.py:23
  777.5 6.0 collective-permute-start.19
Sparse Core Ops, SparseCore 0:
  24.6 101.8 all-reduce.14
  130.0 171.2 all-reduce.12
where the time goes:
time: 795 us; the launch traced here: 794 us
  blocking collectives  382 us (48%)
  waiting for transfers between devices  273 us (34%)
  starting transfers between devices  67.7 us (9%)
  local copies, waits for them, and re-layouts  46.2 us (6%)
  between operations  15.1 us (2%)
  other arithmetic  10.1 us (1%)
    psum x3, blocking collectives, surround(): lat_summed = lax.psum(lat_terms, 'lat')  245 us
    psum x1, waiting for transfers between devices, surround(): lat_summed = lax.psum(lat_terms, 'lat')  175 us
    psum x3, blocking collectives, surround(): lon_summed = lax.psum(lon_terms, 'lon')  137 us
    psum x1, waiting for transfers between devices, surround(): lon_summed = lax.psum(lon_terms, 'lon')  85.8 us
    ppermute x8, starting transfers between devices, padded_2(): lax.ppermute(head, axis, [((i + 1) % count, i) for i in range(ends)])  36 us
    ppermute x8, starting transfers between devices, padded_2(): lax.ppermute(tail, axis, [(i, (i + 1) % count) for i in range(ends)])  21 us
  transfers between devices with their start and end apart: 22, of which 6 were waited for; matrix products, arithmetic and copies ran while one was open for 3% of the time, Pallas kernels for 0%

commit v1 on v0

--- a/solution.py
+++ b/solution.py
@@ -76,7 +76,7 @@
     padded = padded_2(field, (("lat", 0), ("lon", 1)), width)
     lat_terms, lon_terms = rim_terms(field, lat_codes, lat_weights, lon_codes, lon_weights, width)
     lat_summed = lax.psum(lat_terms, "lat")
-    lon_summed = lax.psum(lon_terms, "lon")
+    lon_summed = jnp.sum(jax.lax.all_gather(lon_terms, axis_name="lon"), axis=0)
     arrived = swapped(jnp.concatenate([lat_summed, lon_summed], axis=2), "panel", 0)
     lat_rim = arrived[:, :, :cols_dev]
     lon_rim = arrived[:, :, cols_dev:]

time: 795 us -> 606 us (0.76)
  the two profiles are of different devices: /device:TPU:296 before, /device:TPU:104 now
where the time goes in v1:
time: 606 us; the launch traced here: 605 us
  blocking collectives  294 us (49%)
  waiting for transfers between devices  174 us (29%)
  starting transfers between devices  62.9 us (10%)
  local copies, waits for them, and re-layouts  46.2 us (8%)
  between operations  16.6 us (3%)
  other arithmetic  11.5 us (2%)
    psum x3, blocking collectives, surround(): lat_summed = lax.psum(lat_terms, 'lat')  245 us
    psum x1, waiting for transfers between devices, surround(): lat_summed = lax.psum(lat_terms, 'lat')  142 us
    all_gather x3, blocking collectives, surround(): lon_summed = jnp.sum(jax.lax.all_gather(lon_terms, axis_name='lon'), axis=0)  49.4 us
    ppermute x8, starting transfers between devices, padded_2(): lax.ppermute(head, axis, [((i + 1) % count, i) for i in range(ends)])  31.1 us
    ppermute x8, starting transfers between devices, padded_2(): lax.ppermute(tail, axis, [(i, (i + 1) % count) for i in range(ends)])  20.8 us
    all_gather x1, waiting for transfers between devices, surround(): lon_summed = jnp.sum(jax.lax.all_gather(lon_terms, axis_name='lon'), axis=0)  19.2 us
    gather x16, local copies, waits for them, and re-layouts, rim_terms(): picked = field[jnp.clip(target, 0, rows_dev - 1), cols_at + col_step]  15.7 us
    ppermute x4, waiting for transfers between devices, swapped(): return lax.ppermute(block, axis, route)  12.1 us
  transfers between devices with their start and end apart: 22, of which 6 were waited for; matrix products, arithmetic and copies ran while one was open for 3% of the time, Pallas kernels for 0%

profile of v1, /device:TPU:104, one launch (start us, length us, event | category | flops | bytes accessed | tf_op | source)
XLA Modules:
  0.0 605.0 jit_solution(17411198157895653501)
XLA Ops:
  9.1 1.3 copy_bitcast_fusion
  10.8 0.9 gather_fusion.7
  11.7 0.9 gather_fusion.6
  12.7 0.9 gather_fusion.5
  13.6 0.9 gather_fusion.4
  15.3 3.4 collective-permute-start
  18.8 6.7 %collective-permute-start.1 = (f32[2,32,256]{2,0,1:T(2,128)S(1)}, f32[2,32,256]{2,0,1:T(2,128)S(1)}, u32[]{:S(2)}, u32[]{:S(2)}) collective-permute-start(f32[2,32,256]{2,0,1:T(2,128)S(1)} %get-tuple-element.225), channel_id=1, source_target_pairs={{1,0},{2,1},{3,2},{4,3},{5,4},{6,5},{7,6},{8,7},{9,8},{10,9},{11,1... | collective-permute-start | bytes 196616 | tf_op jit(solution)/shard_map/ppermute | solution.py:23
  26.5 1.3 gather_fusion.3
  27.8 1.3 gather_fusion.2
  29.1 1.3 gather_fusion.1
  30.3 1.3 gather_fusion
  34.9 1.9 collective-permute-start.2
  36.9 3.6 collective-permute-start.3
  40.5 19.2 %all-gather.2.cloned.1.call-done = f32[16,2,2,16,256]{4,3,2,1,0:T(8,128)} async-done(((f32[1,2,2,16,256]{4,3,2,1,0:T(8,128)}), f32[16,2,2,16,256]{4,3,2,1,0:T(8,128)}) %all-gather.2.cloned.1.call-update) | async-done | bytes 1048592 | tf_op jit(solution)/shard_map/all_gather | solution.py:79
  59.8 1.3 reduce_sum.42
  61.1 142.1 %all-reduce.12.cloned.1.call-done = f32[2,2,32,256]{3,2,1,0:T(8,128)} async-done(((f32[2,2,32,256]{3,2,1,0:T(8,128)}), f32[2,2,32,256]{3,2,1,0:T(8,128)}) %all-reduce.12.cloned.1.call-update) | async-done | bytes 131088 | tf_op jit(solution)/shard_map/psum | solution.py:78
  203.2 0.9 pad_maximum_fusion.5
  204.1 3.4 collective-permute-start.4
  208.8 2.8 collective-permute-done.4
  212.0 1.9 dynamic-slice_select_fusion
  213.9 1.6 scatter.54
  218.2 6.0 collective-permute-start.6
  227.0 1.9 collective-permute-start.5
  232.6 17.2 %all_gather.17 = f32[16,2,1,16,128]{4,3,2,1,0:T(8,128)S(1)} all-gather(f32[1,2,1,16,128]{4,3,2,1,0:T(8,128)S(1)} %multiply_add_fusion.7), channel_id=1, replica_groups=mesh['panel'=2,'lon'=16,'lat'=16] {'lon'}, dimensions={0}, use_global_device_ids=true | all-gather | bytes 278528 | tf_op jit(solution)/shard_map/all_gather | solution.py:79
  249.9 82.9 %psum.29 = f32[2,1,32,128]{3,2,1,0:T(8,128)S(1)} all-reduce(f32[2,1,32,128]{3,2,1,0:T(8,128)S(1)} %multiply_add_fusion.4), channel_id=1, replica_groups=mesh['panel'=2,'lon'=16,'lat'=16] {'lat'}, use_global_device_ids=true, to_apply=%region_3.4 | all-reduce | flops 8192 | bytes 65536 | tf_op jit(solution)/shard_map/psum | solution.py:78
  332.9 1.9 collective-permute-start.7
  334.8 3.6 collective-permute-start.8
  338.5 2.5 collective-permute-start.9
  341.1 3.4 collective-permute-done.9
  344.4 1.4 scatter.60
  354.4 1.9 collective-permute-start.11
  356.3 3.9 collective-permute-start.10
  360.3 16.1 %all_gather.18 = f32[16,2,1,16,128]{4,3,2,1,0:T(8,128)S(1)} all-gather(f32[1,2,1,16,128]{4,3,2,1,0:T(8,128)S(1)} %multiply_add_fusion.6), channel_id=1, replica_groups=mesh['panel'=2,'lon'=16,'lat'=16] {'lon'}, dimensions={0}, use_global_device_ids=true | all-gather | bytes 278528 | tf_op jit(solution)/shard_map/all_gather | solution.py:79
  376.5 80.9 %psum.30 = f32[2,1,32,128]{3,2,1,0:T(8,128)S(1)} all-reduce(f32[2,1,32,128]{3,2,1,0:T(8,128)S(1)} %multiply_add_fusion.3), channel_id=1, replica_groups=mesh['panel'=2,'lon'=16,'lat'=16] {'lat'}, use_global_device_ids=true, to_apply=%region_5.6 | all-reduce | flops 8192 | bytes 65536 | tf_op jit(solution)/shard_map/psum | solution.py:78
  457.5 1.9 collective-permute-start.12
  459.4 3.6 collective-permute-start.13
  463.1 2.5 collective-permute-start.14
  465.7 3.4 collective-permute-done.14
  469.0 1.4 scatter.66
  479.0 1.9 collective-permute-start.16
  480.9 3.9 collective-permute-start.15
  484.9 16.1 %all_gather.19 = f32[16,2,1,16,128]{4,3,2,1,0:T(8,128)S(1)} all-gather(f32[1,2,1,16,128]{4,3,2,1,0:T(8,128)S(1)} %multiply_add_fusion.5), channel_id=1, replica_groups=mesh['panel'=2,'lon'=16,'lat'=16] {'lon'}, dimensions={0}, use_global_device_ids=true | all-gather | bytes 278528 | tf_op jit(solution)/shard_map/all_gather | solution.py:79
  501.1 80.9 %psum.31 = f32[2,1,32,128]{3,2,1,0:T(8,128)S(1)} all-reduce(f32[2,1,32,128]{3,2,1,0:T(8,128)S(1)} %multiply_add_fusion.2), channel_id=1, replica_groups=mesh['panel'=2,'lon'=16,'lat'=16] {'lat'}, use_global_device_ids=true, to_apply=%region_7.8 | all-reduce | flops 8192 | bytes 65536 | tf_op jit(solution)/shard_map/psum | solution.py:78
  582.1 1.9 collective-permute-start.17
  584.0 3.6 collective-permute-start.18
  587.7 2.5 collective-permute-start.19
  591.1 2.6 collective-permute-done.19
  593.7 1.4 scatter.74
  (198 shorter events, 37.8 us)
Async XLA Ops:
  8.0 51.8 %all-gather.2.cloned.1.call-start = ((), (), s32[]{:S(2)}) async-start(), calls=%async_computation.1 | async-start | bytes 1114112 | tf_op jit(solution)/shard_map/all_gather | solution.py:79
  8.0 0.7 copy-start.6
  8.1 0.7 copy-start.4
  15.2 187.9 %all-reduce.12.cloned.1.call-start = ((), (), s32[]{:S(2)}) async-start(), calls=%async_computation | async-start | bytes 262144 | tf_op jit(solution)/shard_map/psum | solution.py:78
  15.3 19.6 %collective-permute-start = (f32[2,32,256]{2,0,1:T(2,128)S(1)}, f32[2,32,256]{2,0,1:T(2,128)S(1)}, u32[]{:S(2)}, u32[]{:S(2)}) collective-permute-start(f32[2,32,256]{2,0,1:T(2,128)S(1)} %get-tuple-element.224), channel_id=1, source_target_pairs={{0,1},{1,2},{2,3},{3,4},{4,5},{5,6},{6,7},{7,8},{8,9},{9,10},{10,1... | collective-permute-start | bytes 196616 | tf_op jit(solution)/shard_map/ppermute | solution.py:21
  18.8 16.2 %collective-permute-start.1 = (f32[2,32,256]{2,0,1:T(2,128)S(1)}, f32[2,32,256]{2,0,1:T(2,128)S(1)}, u32[]{:S(2)}, u32[]{:S(2)}) collective-permute-start(f32[2,32,256]{2,0,1:T(2,128)S(1)} %get-tuple-element.225), channel_id=1, source_target_pairs={{1,0},{2,1},{3,2},{4,3},{5,4},{6,5},{7,6},{8,7},{9,8},{10,9},{11,1... | collective-permute-start | bytes 196616 | tf_op jit(solution)/shard_map/ppermute | solution.py:23
  25.4 0.7 copy-start.7
  30.3 1.3 copy-start.5
  32.9 0.7 copy-start.8
  34.9 173.8 %collective-permute-start.2 = (f32[20,2,256]{2,0,1:T(8,128)S(1)}, f32[20,2,256]{2,0,1:T(8,128)S(1)}, u32[]{:S(2)}, u32[]{:S(2)}) collective-permute-start(f32[20,2,256]{2,0,1:T(8,128)S(1)} %get-tuple-element.222), channel_id=1, source_target_pairs={{0,16},{16,32},{32,48},{48,64},{64,80},{80,96},{96,112},{112,128},... | collective-permute-start | bytes 122888 | tf_op jit(solution)/shard_map/ppermute | solution.py:21
  36.9 171.8 %collective-permute-start.3 = (f32[20,2,256]{2,0,1:T(8,128)S(1)}, f32[20,2,256]{2,0,1:T(8,128)S(1)}, u32[]{:S(2)}, u32[]{:S(2)}) collective-permute-start(f32[20,2,256]{2,0,1:T(8,128)S(1)} %get-tuple-element.223), channel_id=1, source_target_pairs={{16,0},{32,16},{48,32},{64,48},{80,64},{96,80},{112,96},{128,112},... | collective-permute-start | bytes 122888 | tf_op jit(solution)/shard_map/ppermute | solution.py:23
  204.1 7.6 %collective-permute-start.4 = (f32[2,2,48,256]{3,2,1,0:T(8,128)S(1)}, f32[2,2,48,256]{3,2,1,0:T(8,128)S(1)}, u32[]{:S(2)}, u32[]{:S(2)}) collective-permute-start(f32[2,2,48,256]{3,2,1,0:T(8,128)S(1)} %pad_maximum_fusion.5), channel_id=1, source_target_pairs={{0,256},{256,0},{1,257},{257,1},{2,258},{258,2},{3,259},{259,3},{4... | collective-permute-start | bytes 589832 | tf_op jit(solution)/shard_map/ppermute | solution.py:37
  216.4 1.0 copy-start
  216.5 1.0 copy-start.1
  218.2 114.7 %collective-permute-start.6 = (f32[1,32,128]{2,0,1:T(1,128)S(1)}, f32[1,32,128]{2,0,1:T(1,128)S(1)}, u32[]{:S(2)}, u32[]{:S(2)}) collective-permute-start(f32[1,32,128]{2,0,1:T(1,128)S(1)} %slice.1083), channel_id=1, source_target_pairs={{1,0},{2,1},{3,2},{4,3},{5,4},{6,5},{7,6},{8,7},{9,8},{10,9},{11,1... | collective-permute-start | bytes 49160 | tf_op jit(solution)/shard_map/ppermute | solution.py:23
  227.0 105.8 %collective-permute-start.5 = (f32[1,32,128]{2,1,0:T(8,128)S(1)}, f32[1,32,128]{2,1,0:T(8,128)S(1)}, u32[]{:S(2)}, u32[]{:S(2)}) collective-permute-start(f32[1,32,128]{2,1,0:T(8,128)S(1)} %slice.1082), channel_id=1, source_target_pairs={{0,1},{1,2},{2,3},{3,4},{4,5},{5,6},{6,7},{7,8},{8,9},{9,10},{10,1... | collective-permute-start | bytes 49160 | tf_op jit(solution)/shard_map/ppermute | solution.py:21
  332.9 8.1 %collective-permute-start.7 = (f32[18,1,128]{2,0,1:T(8,128)S(1)}, f32[18,1,128]{2,0,1:T(8,128)S(1)}, u32[]{:S(2)}, u32[]{:S(2)}) collective-permute-start(f32[18,1,128]{2,0,1:T(8,128)S(1)} %get-tuple-element.230), channel_id=1, source_target_pairs={{0,16},{16,32},{32,48},{48,64},{64,80},{80,96},{96,112},{112,128},... | collective-permute-start | bytes 27656 | tf_op jit(solution)/shard_map/ppermute | solution.py:21
  334.8 6.2 %collective-permute-start.8 = (f32[18,1,128]{2,0,1:T(8,128)S(1)}, f32[18,1,128]{2,0,1:T(8,128)S(1)}, u32[]{:S(2)}, u32[]{:S(2)}) collective-permute-start(f32[18,1,128]{2,0,1:T(8,128)S(1)} %get-tuple-element.231), channel_id=1, source_target_pairs={{16,0},{32,16},{48,32},{64,48},{80,64},{96,80},{112,96},{128,112},... | collective-permute-start | bytes 27656 | tf_op jit(solution)/shard_map/ppermute | solution.py:23
  338.5 6.0 collective-permute-start.9
  346.4 1.0 copy-start.2
  354.4 103.1 %collective-permute-start.11 = (f32[1,32,128]{2,0,1:T(1,128)S(1)}, f32[1,32,128]{2,0,1:T(1,128)S(1)}, u32[]{:S(2)}, u32[]{:S(2)}) collective-permute-start(f32[1,32,128]{2,0,1:T(1,128)S(1)} %slice.1124), channel_id=1, source_target_pairs={{1,0},{2,1},{3,2},{4,3},{5,4},{6,5},{7,6},{8,7},{9,8},{10,9},{11,1... | collective-permute-start | bytes 49160 | tf_op jit(solution)/shard_map/ppermute | solution.py:23
  356.3 101.1 %collective-permute-start.10 = (f32[1,32,128]{2,1,0:T(8,128)S(1)}, f32[1,32,128]{2,1,0:T(8,128)S(1)}, u32[]{:S(2)}, u32[]{:S(2)}) collective-permute-start(f32[1,32,128]{2,1,0:T(8,128)S(1)} %slice.1123), channel_id=1, source_target_pairs={{0,1},{1,2},{2,3},{3,4},{4,5},{5,6},{6,7},{7,8},{8,9},{9,10},{10,1... | collective-permute-start | bytes 49160 | tf_op jit(solution)/shard_map/ppermute | solution.py:21
  457.5 8.1 %collective-permute-start.12 = (f32[18,1,128]{2,0,1:T(8,128)S(1)}, f32[18,1,128]{2,0,1:T(8,128)S(1)}, u32[]{:S(2)}, u32[]{:S(2)}) collective-permute-start(f32[18,1,128]{2,0,1:T(8,128)S(1)} %get-tuple-element.228), channel_id=1, source_target_pairs={{0,16},{16,32},{32,48},{48,64},{64,80},{80,96},{96,112},{112,128},... | collective-permute-start | bytes 27656 | tf_op jit(solution)/shard_map/ppermute | solution.py:21
  459.4 6.2 %collective-permute-start.13 = (f32[18,1,128]{2,0,1:T(8,128)S(1)}, f32[18,1,128]{2,0,1:T(8,128)S(1)}, u32[]{:S(2)}, u32[]{:S(2)}) collective-permute-start(f32[18,1,128]{2,0,1:T(8,128)S(1)} %get-tuple-element.229), channel_id=1, source_target_pairs={{16,0},{32,16},{48,32},{64,48},{80,64},{96,80},{112,96},{128,112},... | collective-permute-start | bytes 27656 | tf_op jit(solution)/shard_map/ppermute | solution.py:23
  463.1 6.0 collective-permute-start.14
  471.0 1.0 copy-start.3
  479.0 103.1 %collective-permute-start.16 = (f32[1,32,128]{2,0,1:T(1,128)S(1)}, f32[1,32,128]{2,0,1:T(1,128)S(1)}, u32[]{:S(2)}, u32[]{:S(2)}) collective-permute-start(f32[1,32,128]{2,0,1:T(1,128)S(1)} %slice.1140), channel_id=1, source_target_pairs={{1,0},{2,1},{3,2},{4,3},{5,4},{6,5},{7,6},{8,7},{9,8},{10,9},{11,1... | collective-permute-start | bytes 49160 | tf_op jit(solution)/shard_map/ppermute | solution.py:23
  480.9 101.1 %collective-permute-start.15 = (f32[1,32,128]{2,1,0:T(8,128)S(1)}, f32[1,32,128]{2,1,0:T(8,128)S(1)}, u32[]{:S(2)}, u32[]{:S(2)}) collective-permute-start(f32[1,32,128]{2,1,0:T(8,128)S(1)} %slice.1139), channel_id=1, source_target_pairs={{0,1},{1,2},{2,3},{3,4},{4,5},{5,6},{6,7},{7,8},{8,9},{9,10},{10,1... | collective-permute-start | bytes 49160 | tf_op jit(solution)/shard_map/ppermute | solution.py:21
  582.1 8.9 %collective-permute-start.17 = (f32[18,1,128]{2,0,1:T(8,128)S(1)}, f32[18,1,128]{2,0,1:T(8,128)S(1)}, u32[]{:S(2)}, u32[]{:S(2)}) collective-permute-start(f32[18,1,128]{2,0,1:T(8,128)S(1)} %get-tuple-element.226), channel_id=1, source_target_pairs={{0,16},{16,32},{32,48},{48,64},{64,80},{80,96},{96,112},{112,128},... | collective-permute-start | bytes 27656 | tf_op jit(solution)/shard_map/ppermute | solution.py:21
  584.0 7.0 %collective-permute-start.18 = (f32[18,1,128]{2,0,1:T(8,128)S(1)}, f32[18,1,128]{2,0,1:T(8,128)S(1)}, u32[]{:S(2)}, u32[]{:S(2)}) collective-permute-start(f32[18,1,128]{2,0,1:T(8,128)S(1)} %get-tuple-element.227), channel_id=1, source_target_pairs={{16,0},{32,16},{48,32},{64,48},{80,64},{96,80},{112,96},{128,112},... | collective-permute-start | bytes 27656 | tf_op jit(solution)/shard_map/ppermute | solution.py:23
  587.7 6.0 collective-permute-start.19
Sparse Core Ops, SparseCore 0:
  15.4 44.3 all-gather.1
Sparse Core Ops, SparseCore 1:
  32.6 170.5 all-reduce.11
